TPU v7x, 512 devices: a whole 4x8x8 slice. The times are simulated.
512 devices in a mesh: freq: 4 (over z_lo), px: 16 (over z_hi, y), py: 8 (over x, core).
Axes of the slice: x: 4, y: 8, z: 8 (z_hi: 2, z_lo: 4; z = z_hi * 4 + z_lo), core: 2. Of those that a mesh axis runs over, the one named last changes fastest.
Arguments:
- observed: float32 [4, 512, 2, 128], P('freq', ('px', 'py')), may hold values from -6 to 6
- noise_scale: float32 [4, 512], P('freq', ('px', 'py')), may hold values from 0.5 to 2
- forward_kernel: bfloat16 [4, 128, 512, 2, 512], P('freq', 'px', 'py'), may hold values from -0.03125 to 0.03125
- model_field: float32 [128, 512, 128], P('px', 'py'), may hold values from -6 to 6
- classes: int32 [128, 512], P('px', 'py'), may hold values from 0 to 15
- kappa_table: float32 [16], replicated, may hold values from 0.1 to 0.6
- coupling_table: float32 [4, 16], replicated, may hold values from 0.15 to 0.35
Outputs:
- weighted_residual: float32 [4, 512, 2, 128], P('freq', ('px', 'py'))
- gradient: float32 [128, 512, 128], P('px', 'py')
All inputs are finite; a program needn't handle non-finite values.
Results may differ from a plain program's by a relative error of at most 0.003.
Values may be sent and summed in bfloat16 or wider, within the bound.
A program may use at most 64 MiB of HBM per device.

v0:
```python
import jax
import jax.numpy as jnp
from jax import lax
from jax.sharding import PartitionSpec as P

SWEEPS = 4


FREEDOM = 4.0
PRIOR_WEIGHT = 0.04


def with_halo(shard, sides, width):
    for axis, dim in sides:
        peers, length = (lax.axis_size(axis), shard.shape[dim])
        up = [(i, (i + 1) % peers) for i in range(peers - 1)]
        down = [(j, i) for i, j in up]
        last = lax.slice_in_dim(shard, length - width, length, axis=dim)
        initial = lax.slice_in_dim(shard, 0, width, axis=dim)
        before = lax.ppermute(last, axis, up)
        after = lax.ppermute(initial, axis, down)
        shard = jnp.concatenate([before, shard, after], axis=dim)
    return shard


def student_weights(misfit, noise):
    inverse = 1.0 / (noise * noise)
    spread = (misfit[:, 0] * misfit[:, 0] + misfit[:, 1] * misfit[:, 1]) * inverse[:, None]
    factor = (FREEDOM + 2.0) / (FREEDOM + spread) * inverse[:, None]
    return misfit * factor[:, None, :]


def coefficients(classes, kappa_table, coupling_table):
    levels = jnp.arange(kappa_table.shape[0], dtype=jnp.int32)
    onehot = (classes[..., None] == levels).astype(jnp.float32)
    diagonal = kappa_table + jnp.sum(coupling_table, axis=0)
    class_table = jnp.concatenate([diagonal[None, :], coupling_table], axis=0)
    return jnp.einsum("xyk,ck->xyc", onehot, class_table, precision=lax.Precision.HIGHEST)


def operate(padded, coefficient):
    center = padded[1:-1, 1:-1]
    beside = coefficient[..., 1:2] * padded[:-2, 1:-1] + coefficient[..., 2:3] * padded[2:, 1:-1]
    beside = (
        beside
        + coefficient[..., 3:4] * padded[1:-1, :-2]
        + coefficient[..., 4:5] * padded[1:-1, 2:]
    )
    return coefficient[..., 0:1] * center - beside


def prior_sweeps(state_field, coefficient):
    for sweep_index in range(SWEEPS):
        padded = with_halo(state_field, (("px", 0), ("py", 1)), 1)
        state_field = operate(padded, coefficient)
    return state_field


def local(observed, noise_scale, forward_kernel, model_field, classes, kappa_table, coupling_table):
    kernel_flat = forward_kernel.reshape(-1, forward_kernel.shape[3], forward_kernel.shape[4])
    realizations = model_field.shape[2]
    cells = kernel_flat.shape[0]
    model_low = model_field.astype(jnp.bfloat16).reshape(cells, realizations)
    kernel_part = kernel_flat
    predicted = lax.psum_scatter(
        jnp.einsum("pcs,pr->scr", kernel_part, model_low, preferred_element_type=jnp.float32),
        ("px", "py"),
        scatter_dimension=0,
        tiled=True,
    )
    weighted = student_weights(predicted - observed[0], noise_scale[0])
    weighted_low = weighted.astype(jnp.bfloat16)
    kernel_part = kernel_flat
    data_grad = jnp.einsum(
        "pcs,scr->pr",
        kernel_part,
        lax.all_gather(weighted_low, ("px", "py"), axis=0, tiled=True),
        preferred_element_type=jnp.float32,
    )
    data_grad = data_grad.reshape(model_field.shape)
    coefficient = coefficients(classes, kappa_table, coupling_table)
    data_total = lax.psum(data_grad, "freq")
    prior_term = prior_sweeps(model_field, coefficient)
    gradient = data_total + PRIOR_WEIGHT * prior_term
    return (weighted[None], gradient)


def solution(mesh):
    in_specs = (
        P("freq", ("px", "py"), None, None),
        P("freq", ("px", "py")),
        P("freq", "px", "py", None, None),
        P("px", "py", None),
        P("px", "py"),
        P(),
        P(),
    )
    out_specs = (P("freq", ("px", "py"), None, None), P("px", "py", None))
    return jax.shard_map(local, mesh=mesh, in_specs=in_specs, out_specs=out_specs, check_vma=False)
```

profile of v0, /device:TPU:1, one launch (start us, length us, event | category | flops | bytes accessed | tf_op | source)
XLA Modules:
  0.0 1826.6 jit_solution(14321190208286012507)
XLA Ops:
  7.2 0.9 fusion.50
  8.1 4.2 collective-permute-start
  12.3 1.3 collective-permute-start.1
  13.8 1.0 constant_dynamic-update-slice_fusion.1
  14.8 2.1 collective-permute-done.1
  16.9 7.2 collective-permute-start.3
  24.1 1.9 collective-permute-start.2
  26.1 1.1 collective-permute-done.2
  27.6 1.3 collective-permute-start.5
  28.9 4.0 collective-permute-start.4
  32.9 1.0 collective-permute-done.4
  33.9 3.2 collective-permute-start.7
  37.1 3.6 collective-permute-start.6
  40.8 0.7 collective-permute-done.6
  42.0 1.3 collective-permute-start.9
  43.3 4.6 collective-permute-start.8
  48.2 1.0 copy.31
  49.3 1.9 collective-permute-start.11
  51.3 4.6 collective-permute-start.10
  55.9 1.3 dynamic-slice
  58.2 1492.3 %all-reduce.6.cloned.1.call-done = f32[512,2,128]{2,1,0:T(2,128)} async-done(((f32[512,2,128]{2,1,0:T(2,128)}), f32[512,2,128]{2,1,0:T(2,128)}) %all-reduce.6.cloned.1.call-update) | async-done | bytes 524304
  1550.5 0.7 constant_dynamic-slice_fusion
  1551.3 218.0 %all_gather.3 = bf16[512,2,128]{2,1,0:T(2,128)(2,1)S(1)} all-gather(bf16[4,2,128]{2,1,0:T(2,128)(2,1)S(1)} %copy.34), channel_id=1, replica_groups=mesh['freq'=4,'px'=16,'py'=8] {'px','py'}, dimensions={0}, use_global_device_ids=true | all-gather | bytes 264192 | tf_op jit(solution)/shard_map/all_gather | solution.py:77
  1769.8 0.8 copy.37
  1770.7 1.3 collective-permute-start.13
  1772.0 4.0 collective-permute-start.12
  1776.0 1.0 collective-permute-done.12
  1777.0 3.2 collective-permute-start.15
  1780.2 3.1 collective-permute-start.14
  1783.3 0.6 copy.38
  1784.0 33.7 %all-reduce.4.cloned.1.call-done = f32[8,64,128]{2,1,0:T(8,128)} async-done(((f32[8,64,128]{2,1,0:T(8,128)}), f32[8,64,128]{2,1,0:T(8,128)}) %all-reduce.4.cloned.1.call-update) | async-done | bytes 262160 | tf_op jit(solution)/shard_map/psum | solution.py:82
  1817.7 2.1 fusion.6
  (52 shorter events, 2.7 us)
Async XLA Ops:
  7.2 40.7 %copy-start = (bf16[1,8,64,2,512]{4,3,2,1,0:T(2,128)(2,1)S(1)}, bf16[1,8,64,2,512]{4,3,2,1,0:T(2,128)(2,1)}, u32[]{:S(2)}) copy-start(bf16[1,8,64,2,512]{4,3,2,1,0:T(2,128)(2,1)} %param.9) | copy-start | bytes 3145732
  7.2 1543.4 %all-reduce.6.cloned.1.call-start = ((), (), s32[]{:S(2)}) async-start(), calls=%async_computation.1 | async-start | bytes 1048576
  8.1 5.5 copy-start.2
  8.1 5.5 copy-start.3
  8.1 5.7 collective-permute-start
  12.3 1.3 copy-start.5
  12.3 4.7 collective-permute-start.1
  13.8 13.4 copy-start.1
  16.9 9.1 collective-permute-start.3
  24.1 3.1 collective-permute-start.2
  27.6 5.3 collective-permute-start.5
  28.9 5.0 collective-permute-start.4
  33.9 6.9 collective-permute-start.7
  37.1 4.4 collective-permute-start.6
  42.0 7.3 collective-permute-start.9
  43.3 6.0 collective-permute-start.8
  49.2 1768.5 %all-reduce.4.cloned.1.call-start = ((), (), s32[]{:S(2)}) async-start(), calls=%async_computation | async-start | bytes 524288 | tf_op jit(solution)/shard_map/psum | solution.py:82
  49.3 6.5 copy-start.6
  49.3 8.5 collective-permute-start.11
  51.3 6.5 collective-permute-start.10
  58.2 1493.0 %copy-start.4 = (f32[1,4,2,128]{3,2,1,0:T(2,128)S(1)}, f32[1,4,2,128]{3,2,1,0:T(2,128)}, u32[]{:S(2)}) copy-start(f32[1,4,2,128]{3,2,1,0:T(2,128)} %param.7) | copy-start | bytes 12292
  1770.7 5.3 collective-permute-start.13
  1772.0 5.0 collective-permute-start.12
  1777.0 6.9 collective-permute-start.15
  1780.2 3.8 collective-permute-start.14
Sparse Core Ops, SparseCore 0:
  49.4 1501.1 all-reduce.5
  1770.8 46.8 all-reduce.3
where the time goes:
time: 1830 us
  waiting for transfers between devices  1530 us (84%)
  blocking collectives  218 us (12%)
  starting transfers between devices  50.6 us (3%)
    unnamed x3, waiting for transfers between devices  1490 us
    all_gather x1, blocking collectives, local(): lax.all_gather(weighted_low, ('px', 'py'), axis=0, tiled=True)  218 us
  transfers between devices with their start and end apart: 18, of which 8 were waited for; matrix products, arithmetic and copies ran while one was open for 0% of the time, Pallas kernels for 0%

commit v1 on v0

v1 whole, which is shorter than its diff:
```python
import functools

import jax
import jax.numpy as jnp
from jax import lax
from jax.experimental import pallas as pl
from jax.experimental.pallas import tpu as pltpu
from jax.sharding import PartitionSpec as P

SWEEPS = 4
FREEDOM = 4.0
PRIOR_WEIGHT = 0.04
MESH = pl.DeviceIdType.MESH
F32, BF16 = jnp.float32, jnp.bfloat16

NF, NZ, NY_CHIP, NX_CHIP = 4, 2, 8, 4


def rolled(v, shift, axis):
    return pltpu.roll(v, shift % v.shape[axis], axis)


def kernel(
    k_hbm, m_hbm, obs_hbm, noise_hbm, cls_hbm, kappa_hbm, coup_hbm,
    wout, gout,
    kscr, ext, obs_v, noise_v, cls_in, kappa_v, coup_v,
    mx, p, cin, onout, onin, xin, b, yin, zout, zin, wf, wt, wtin,
    g, fsend, fin, fown, va, vb, coef, cls,
    lsem, csem, xsem, ysem, zsem, osem, aysem, axsem, acsem, tsem, rsem, gsem, hsem,
):
    f = lax.axis_index("freq")
    px = lax.axis_index("px")
    py = lax.axis_index("py")
    zh, y = px // NY_CHIP, px % NY_CHIP
    x, c = py // 2, py % 2

    def dev(f=f, zh=zh, y=y, x=x, c=c):
        return {"freq": f, "px": zh * NY_CHIP + y, "py": x * 2 + c}

    partner = dev(c=1 - c)
    x_peers = [dev(x=(x + d) % NX_CHIP) for d in range(1, NX_CHIP)]
    y_peers = [dev(y=(y + d) % NY_CHIP) for d in range(1, NY_CHIP)]
    z_peer = dev(zh=1 - zh)
    f_peers = [dev(f=(f + d) % NF) for d in range(1, NF)]
    npx, npy = NZ * NY_CHIP, NX_CHIP * 2
    above = {"freq": f, "px": (px + npx - 1) % npx, "py": py}
    below = {"freq": f, "px": (px + 1) % npx, "py": py}
    left = {"freq": f, "px": px, "py": (py + npy - 1) % npy}
    right = {"freq": f, "px": px, "py": (py + 1) % npy}

    def load(src, dst, i):
        copy = pltpu.make_async_copy(src, dst, lsem.at[i])
        copy.start()
        return copy

    m_load = load(m_hbm, ext.at[4:12, 8:72], 0)
    k_loads = [load(k_hbm.at[:, :, pl.ds(lb * 128, 128)], kscr.at[lb], 1 + lb) for lb in range(4)]
    small = [
        load(obs_hbm, obs_v, 5), load(noise_hbm, noise_v, 6), load(cls_hbm, cls_in.at[1, 8:16], 7),
        load(kappa_hbm, kappa_v, 8), load(coup_hbm, coup_v, 9),
    ]

    bar = pltpu.get_barrier_semaphore()
    greeted = [partner, left, right, z_peer, above, below] + x_peers + y_peers + f_peers
    for peer in greeted:
        pl.semaphore_signal(bar, inc=1, device_id=peer, device_id_type=MESH)

    def remote(src, dst, sems, i, peer):
        return pltpu.make_async_remote_copy(
            src_ref=src, dst_ref=dst, send_sem=sems.at[0, i], recv_sem=sems.at[1, i],
            device_id=peer, device_id_type=MESH,
        )

    lane = lax.broadcasted_iota(jnp.int32, (8, 128), 1)
    sub = lax.broadcasted_iota(jnp.int32, (8, 128), 0)

    m_load.wait()
    m = ext[4:12, 8:72, :].reshape(512, 128)
    low = lax.broadcasted_iota(jnp.int32, (512, 128), 1) < 64
    mr = rolled(m, 64, 1)
    mx.at[0][pl.ds(0, 512, stride=2), :] = jnp.where(low, m, 0.0)
    mx.at[0][pl.ds(1, 512, stride=2), :] = jnp.where(low, 0.0, mr)
    mx.at[1][pl.ds(0, 512, stride=2), :] = jnp.where(low, mr, 0.0)
    mx.at[1][pl.ds(1, 512, stride=2), :] = jnp.where(low, 0.0, m)
    model = jnp.concatenate([mx[0].astype(BF16), mx[1].astype(BF16)], axis=1)

    for copy in small:
        copy.wait()
    even = obs_v[pl.ds(0, 4, stride=2), :]
    odd = obs_v[pl.ds(1, 4, stride=2), :]
    lo4 = lax.broadcasted_iota(jnp.int32, (4, 128), 1) < 64
    mine = (sub // 4) == c
    obs_tiles = []
    for t in (jnp.where(lo4, even, rolled(odd, 64, 1)), jnp.where(lo4, rolled(even, 64, 1), odd)):
        obs_tiles.append(jnp.where(mine, jnp.concatenate([t, t], axis=0), 0.0))
    nrow = jnp.broadcast_to(noise_v[...], (8, 4))
    pick = lax.broadcasted_iota(jnp.int32, (8, 4), 1) == lax.broadcasted_iota(jnp.int32, (8, 4), 0) - c * 4
    noise_tile = jnp.broadcast_to(jnp.sum(jnp.where(pick, nrow, 0.0), axis=1, keepdims=True), (8, 128))
    onout[0] = jnp.where(c == 0, obs_tiles[1], obs_tiles[0])
    onout[1] = noise_tile
    obs_own = jnp.where(c == 0, obs_tiles[0], obs_tiles[1])

    c_copies = []
    for lb in range(4):
        k_loads[lb].wait()
        kv = kscr.at[lb].reshape(1024, 128)[...]
        part = lax.dot_general(kv, model, (((0,), (0,)), ((), ())), preferred_element_type=F32)
        rows = pl.ds(lb * 4, 4)
        p[0, rows] = part[:, :128].reshape(4, 4, 8, 128)
        p[1, rows] = part[:, 128:].reshape(4, 4, 8, 128)
        if lb == 0:
            pl.semaphore_wait(bar, len(greeted))
        copy = remote(p.at[1 - c, rows], cin.at[rows], csem, lb, partner)
        copy.start()
        c_copies.append(copy)
    on_copy = remote(onout, onin, osem, 0, partner)
    on_copy.start()

    x_copies = []
    for lb in range(4):
        rows = pl.ds(lb * 4, 4)
        c_copies[lb].wait_recv()
        p[c, rows] = p[c, rows] + cin[rows]
        for d in range(1, NX_CHIP):
            copy = remote(
                p.at[c, rows, (x + d) % NX_CHIP], xin.at[d - 1, rows], xsem, (d - 1) * 4 + lb, x_peers[d - 1]
            )
            copy.start()
            x_copies.append(copy)

    upper = f < 2
    src_row = jnp.where(upper, 8, 4)
    dst_row = jnp.where(upper, 0, 12)
    v_peer = {"freq": f, "px": (px + jnp.where(upper, 1, npx - 1)) % npx, "py": py}
    v_copies = [
        remote(ext.at[pl.ds(src_row, 4), 8:72], ext.at[pl.ds(dst_row, 4), 8:72], hsem, 0, v_peer),
        remote(
            cls_in.at[1, 8:16], cls_in.at[1, pl.ds(pl.multiple_of(jnp.where(upper, 0, 16), 8), 8)],
            hsem, 1, v_peer,
        ),
    ]
    for copy in v_copies:
        copy.start()

    for copy in x_copies:
        copy.wait_recv()
    b[...] = (p[c, :, x] + xin[0] + (xin[1] + xin[2])).reshape(NZ, NY_CHIP, 8, 128)

    y_copies = []
    for d in range(1, NY_CHIP):
        copy = remote(b.at[:, (y + d) % NY_CHIP], yin.at[d - 1], ysem, d - 1, y_peers[d - 1])
        copy.start()
        y_copies.append(copy)

    for copy in v_copies:
        copy.wait_recv()
    rows10 = pl.ds(2 * f, 10)
    rows16 = pl.ds(pl.multiple_of(jnp.where(upper, 0, 8), 8), 16)
    h_copies = [
        remote(ext.at[rows10, 8:16], ext.at[rows10, 72:80], hsem, 2, left),
        remote(ext.at[rows10, 64:72], ext.at[rows10, 0:8], hsem, 3, right),
        remote(cls_in.at[1, rows16], cls_in.at[2, rows16], hsem, 4, left),
        remote(cls_in.at[1, rows16], cls_in.at[0, rows16], hsem, 5, right),
    ]
    for copy in h_copies:
        copy.start()

    on_copy.wait_recv()
    noise_chip = noise_tile + onin[1]
    obs_chip = obs_own + onin[0]

    for copy in y_copies:
        copy.wait_recv()
    s01, s23, s45 = yin[0] + yin[1], yin[2] + yin[3], yin[4] + yin[5]
    d_sum = (b[:, y] + yin[6]) + (s01 + s23) + s45
    for zi in range(NZ):
        zout[zi] = d_sum[zi] - jnp.where(zh == zi, obs_chip, 0.0)
    zout[2] = noise_chip

    z_copy = remote(zout, zin, zsem, 0, z_peer)
    z_copy.start()
    z_copy.wait_recv()

    w_own = jnp.zeros((8, 128), F32)
    for zi in range(NZ):
        misfit = zout[zi] + zin[zi]
        noise = jnp.where(zh == zi, noise_chip, zin[2])
        inverse = 1.0 / (noise * noise)
        square = misfit * misfit
        spread = (square + rolled(square, 64, 1)) * inverse
        weighted = misfit * ((FREEDOM + 2.0) / (FREEDOM + spread) * inverse)
        wf[c, zi, y, x] = weighted.astype(BF16)
        w_own = jnp.where(zh == zi, weighted, w_own)
    wt[...] = w_own

    ay_copies = []
    for d in range(1, NY_CHIP):
        copy = remote(wf.at[c, :, y, x], wf.at[c, :, y, x], aysem, d - 1, y_peers[d - 1])
        copy.start()
        ay_copies.append(copy)
    t_copy = remote(wt, wtin, tsem, 0, partner)
    t_copy.start()

    for copy in h_copies:
        copy.wait_recv()
    blocks = []
    for blk in range(3):
        rows = [cls_in[blk, 5 + 2 * i: 13 + 2 * i, :] for i in range(NF)]
        v = jnp.where(f == 0, rows[0], jnp.where(f == 1, rows[1], jnp.where(f == 2, rows[2], rows[3])))
        blocks.append(jnp.concatenate([v, v], axis=1))
    here = jnp.where(lane < 8, rolled(blocks[0], 72, 1), jnp.where(lane < 72, rolled(blocks[1], 8, 1), rolled(blocks[2], 72, 1)))
    grow = px * 8 + 2 * f - 3 + sub
    gcol = py * 64 + lane - 8
    ok = (grow >= 0) & (grow < npx * 8) & (gcol >= 0) & (gcol < npy * 64) & (lane < 80)
    cls[...] = jnp.where(ok, here, -1)

    eye = lax.broadcasted_iota(jnp.int32, (16, 16), 0) == lax.broadcasted_iota(jnp.int32, (16, 16), 1)

    def column(row):
        spread_row = jnp.where(eye, jnp.broadcast_to(row, (16, 16)), 0.0)
        return jnp.broadcast_to(jnp.sum(spread_row, axis=1, keepdims=True), (16, 128))

    coup = [column(coup_v[i:i + 1, :]) for i in range(4)]
    diagonal = column(kappa_v[...]) + (coup[0] + coup[1] + coup[2] + coup[3])
    table = jnp.concatenate([diagonal] + coup, axis=1)
    high = table.astype(BF16)
    rest = table - high.astype(F32)
    mid = rest.astype(BF16)
    tail = (rest - mid.astype(F32)).astype(BF16)
    table3 = jnp.concatenate([high, mid, tail], axis=0)
    level = lax.broadcasted_iota(jnp.int32, (48, 128), 0) % 16
    for k in range(8):
        onehot = (jnp.broadcast_to(cls[k:k + 1, :], (48, 128)) == level).astype(F32).astype(BF16)
        rows = lax.dot_general(onehot, table3, (((0,), (0,)), ((), ())), preferred_element_type=F32)
        for q in range(5):
            coef[k, q] = rows[:80, q * 128:(q + 1) * 128]

    c_row = px * 8 + 2 * f - 4
    col80 = lax.broadcasted_iota(jnp.int32, (80, 128), 0) + (py * 64 - 8)
    col_ok = (col80 >= 0) & (col80 < npy * 64)

    def fill(i, carry):
        row_ok = (c_row + i >= 0) & (c_row + i < npx * 8)
        va[i] = jnp.where(col_ok & row_ok, ext[2 * f + i], 0.0)
        return carry

    lax.fori_loop(0, 10, fill, 0)

    src, dst = va, vb
    for sweep in range(SWEEPS):
        def row_step(i, carry, src=src, dst=dst):
            center = src[i]
            beside = coef[i - 1, 1] * src[i - 1] + coef[i - 1, 2] * src[i + 1]
            beside = beside + coef[i - 1, 3] * rolled(center, 1, 0) + coef[i - 1, 4] * rolled(center, -1, 0)
            dst[i] = coef[i - 1, 0] * center - beside
            return carry

        lax.fori_loop(1 + sweep, 9 - sweep, row_step, 0)
        src, dst = dst, src
    prior = PRIOR_WEIGHT * src[4:6, 8:72, :].reshape(128, 128)
    fown[...] = prior

    for copy in ay_copies:
        copy.wait_recv()
    own_x = wf.at[c, :, :, x]
    ax_copies = []
    for d in range(1, NX_CHIP):
        copy = remote(own_x, own_x, axsem, d - 1, x_peers[d - 1])
        copy.start()
        ax_copies.append(copy)
    ac_copies = [remote(own_x, own_x, acsem, 0, partner)]
    ac_copies[0].start()
    for d in (1, 3, 2):
        ax_copies[d - 1].wait_recv()
        from_x = wf.at[c, :, :, (x + NX_CHIP - d) % NX_CHIP]
        copy = remote(from_x, from_x, acsem, d, partner)
        copy.start()
        ac_copies.append(copy)

    t_copy.wait_recv()
    other = wtin[...]
    half0 = jnp.where(c == 0, w_own, other)
    half1 = jnp.where(c == 0, other, w_own)
    half0 = jnp.where(c == 0, half0[0:4], half0[4:8])
    half1 = jnp.where(c == 0, half1[0:4], half1[4:8])
    wout[pl.ds(0, 4, stride=2), :] = jnp.where(lo4, half0, rolled(half1, 64, 1))
    wout[pl.ds(1, 4, stride=2), :] = jnp.where(lo4, rolled(half0, 64, 1), half1)

    for copy in ac_copies:
        copy.wait_recv()
    weights = jnp.concatenate(
        [wf.at[h].reshape(512, 128)[...] for h in range(2)], axis=1
    )

    lo128 = lax.broadcasted_iota(jnp.int32, (128, 128), 1) < 64
    r_copies = []
    for d in (2, 3, 1, 0):
        q = (f + d) % NF
        rows = pl.ds(pl.multiple_of(q * 256, 256), 256)
        kq = jnp.concatenate([kscr.at[lb].reshape(1024, 128)[rows, :] for lb in range(4)], axis=1)
        both = jnp.dot(kq, weights, preferred_element_type=F32)
        g[0] = both[:, :128]
        g[1] = both[:, 128:]
        e0, o0 = g.at[0][pl.ds(0, 128, stride=2), :], g.at[0][pl.ds(1, 128, stride=2), :]
        e1, o1 = g.at[1][pl.ds(0, 128, stride=2), :], g.at[1][pl.ds(1, 128, stride=2), :]
        grad = jnp.where(lo128, e0, o1) + rolled(jnp.where(lo128, e1, o0), 64, 1)
        if d:
            fsend[d - 1] = grad.astype(BF16)
            copy = remote(fsend.at[d - 1], fin.at[d - 1], rsem, d - 1, f_peers[d - 1])
            copy.start()
            r_copies.append(copy)
        else:
            total = grad + fown[...]
    for copy in r_copies:
        copy.wait_recv()
    total = total + (fin[0].astype(F32) + fin[1].astype(F32)) + fin[2].astype(F32)
    fsum = fsend.at[3]
    fsum[...] = total.astype(BF16)
    own = pltpu.make_async_copy(fsum, gout.at[f], lsem.at[10])
    own.start()
    g_copies = []
    for d in range(1, NF):
        copy = remote(fsum, gout.at[f], gsem, d - 1, f_peers[d - 1])
        copy.start()
        g_copies.append(copy)
    for copy in g_copies:
        copy.wait_recv()
    own.wait()
    everything = (
        c_copies + [on_copy] + x_copies + v_copies + y_copies + h_copies + [z_copy] + ay_copies
        + [t_copy] + ax_copies + ac_copies + r_copies + g_copies
    )
    for copy in everything:
        copy.wait_send()


def local(observed, noise_scale, forward_kernel, model_field, classes, kappa_table, coupling_table):
    vmem = lambda shape, dtype=F32: pltpu.VMEM(shape, dtype)
    sems = lambda n: pltpu.SemaphoreType.DMA((2, n))
    weighted, grad = pl.pallas_call(
        kernel,
        name="gauss_newton",
        out_shape=(
            jax.ShapeDtypeStruct((8, 128), F32),
            jax.ShapeDtypeStruct((NF, 128, 128), BF16),
        ),
        in_specs=[pl.BlockSpec(memory_space=pl.ANY)] * 7,
        out_specs=(pl.BlockSpec(memory_space=pltpu.VMEM), pl.BlockSpec(memory_space=pl.ANY)),
        scratch_shapes=[
            vmem((4, 512, 2, 128), BF16), vmem((16, 80, 128)), vmem((8, 128)), vmem((1, 4)),
            vmem((3, 24, 64), jnp.int32), vmem((1, 16)), vmem((4, 16)),
            vmem((2, 1024, 128)), vmem((2, 16, 4, 8, 128)), vmem((16, 4, 8, 128)), vmem((2, 8, 128)), vmem((2, 8, 128)),
            vmem((3, 16, 8, 128)), vmem((2, 8, 8, 128)), vmem((7, 2, 8, 128)), vmem((3, 8, 128)), vmem((3, 8, 128)),
            vmem((2, 2, 8, 4, 8, 128), BF16), vmem((8, 128)), vmem((8, 128)),
            vmem((2, 256, 128)), vmem((4, 128, 128), BF16), vmem((3, 128, 128), BF16), vmem((128, 128)),
            vmem((10, 80, 128)), vmem((10, 80, 128)), vmem((8, 5, 80, 128)), vmem((8, 128), jnp.int32),
            pltpu.SemaphoreType.DMA((11,)), sems(4), sems(12), sems(7), sems(1), sems(1), sems(7), sems(3), sems(4),
            sems(1), sems(3), sems(3), sems(6),
        ],
        compiler_params=pltpu.CompilerParams(
            collective_id=0, has_side_effects=True, vmem_limit_bytes=48 * 1024 * 1024
        ),
    )(
        forward_kernel.reshape(512, 2, 512),
        model_field,
        observed.reshape(8, 128),
        noise_scale,
        classes,
        kappa_table.reshape(1, 16),
        coupling_table,
    )
    return weighted.reshape(observed.shape), grad.astype(F32).reshape(model_field.shape)


def solution(mesh):
    in_specs = (
        P("freq", ("px", "py"), None, None),
        P("freq", ("px", "py")),
        P("freq", "px", "py", None, None),
        P("px", "py", None),
        P("px", "py"),
        P(),
        P(),
    )
    out_specs = (P("freq", ("px", "py"), None, None), P("px", "py", None))
    return jax.shard_map(local, mesh=mesh, in_specs=in_specs, out_specs=out_specs, check_vma=False)
```

time: 1830 us -> 57.6 us (0.03)
  waiting for transfers between devices: 1530 us -> 0 us
  blocking collectives: 218 us -> 0 us
  Pallas kernels: 0 us -> 51.2 us
  starting transfers between devices: 50.6 us -> 0 us
    unnamed x3 -> x0, waiting for transfers between devices: 1490 us -> none
    all_gather x1 -> x0, blocking collectives: 218 us -> none  [local(): lax.all_gather(weighted_low, ('px', 'py'), axis=0, tiled=True)]
    pallas_call x0 -> x1, Pallas kernels: none -> 51.2 us  [local(): pl.pallas_call(kernel, name='gauss_newton', out_shape=(jax.ShapeDtypeStru...]
    ppermute x16 -> x0, starting transfers between devices: 50.6 us -> none  [the longest x8 29.9 us: with_halo(): before = lax.ppermute(last, axis, up)]
    psum x1 -> x0, waiting for transfers between devices: 33.7 us -> none  [local(): data_total = lax.psum(data_grad, 'freq')]
  transfers between devices with their start and end apart: 18 -> 0, of which waited for: 8 -> 0; matrix products, arithmetic and copies ran while one was open for 0% -> 0% of each run, Pallas kernels for 0% -> 0%
where the time goes in v1:
time: 57.6 us; the launch traced here: 57.3 us
  Pallas kernels  51.2 us (89%)
  local copies, waits for them, and re-layouts  4.8 us (8%)
  other arithmetic  0.72 us (1%)
  between operations  0.67 us (1%)
    pallas_call x1, Pallas kernels, local(): pl.pallas_call(kernel, name='gauss_newton', out_shape=(jax.ShapeDtypeStru...  51.2 us
    unnamed x15, local copies, waits for them, and re-layouts  4.8 us

profile of v1, /device:TPU:1, one launch (start us, length us, event | category | flops | bytes accessed | tf_op | source)
XLA Modules:
  0.0 57.3 jit_solution(2574149643902099330)
XLA Ops:
  0.6 0.0 copy-start.2
  0.6 0.0 copy-start.5
  0.7 0.0 copy-start.6
  0.7 0.7 %copy-done.2 = f32[1,4,2,128]{3,2,1,0:T(2,128)S(1)} copy-done((f32[1,4,2,128]{3,2,1,0:T(2,128)S(1)}, f32[1,4,2,128]{3,2,1,0:T(2,128)}, u32[]{:S(2)}) %copy-start.2) | copy-done | bytes 4120
  1.3 0.0 copy-done.5
  1.3 0.0 copy-done.6
  1.3 0.0 copy-start
  1.3 1.2 %copy-done = bf16[1,8,64,2,512]{4,3,2,1,0:T(2,128)(2,1)S(1)} copy-done((bf16[1,8,64,2,512]{4,3,2,1,0:T(2,128)(2,1)S(1)}, bf16[1,8,64,2,512]{4,3,2,1,0:T(2,128)(2,1)}, u32[]{:S(2)}) %copy-start) | copy-done | bytes 1048600
  2.6 0.0 copy-start.1
  2.6 0.9 %copy-done.1 = f32[8,64,128]{2,1,0:T(8,128)S(1)} copy-done((f32[8,64,128]{2,1,0:T(8,128)S(1)}, f32[8,64,128]{2,1,0:T(8,128)}, u32[]{:S(2)}) %copy-start.1) | copy-done | bytes 262168
  3.5 0.0 copy-start.3
  3.5 0.7 %copy-done.3 = s32[8,64]{1,0:T(8,128)S(1)} copy-done((s32[8,64]{1,0:T(8,128)S(1)}, s32[8,64]{1,0:T(8,128)}, u32[]{:S(2)}) %copy-start.3) | copy-done | bytes 2072
  4.2 0.0 copy-start.4
  4.2 0.7 %copy-done.4 = f32[4,16]{1,0:T(4,128)S(1)} copy-done((f32[4,16]{1,0:T(4,128)S(1)}, f32[4,16]{1,0:T(4,128)}, u32[]{:S(2)}) %copy-start.4) | copy-done | bytes 280
  4.9 51.2 %gauss_newton.1 = (f32[8,128]{1,0:T(8,128)S(1)}, bf16[4,128,128]{2,1,0:T(8,128)(2,1)S(1)}) custom-call(bf16[512,2,512]{2,1,0:T(2,128)(2,1)S(1)} %bitcast.6, f32[8,64,128]{2,1,0:T(8,128)S(1)} %copy-done.1, f32[8,128]{1,0:T(8,128)S(1)} %bitcast.8, f32[1,4]{1,0:T(1,128)S(1)} %copy-done.5, s32[8,64]{1,0:T(8,128)S(1)} %copy-done.3, f32[1,16]{1,0:T(1,128)S(1)} %bitcast.10, ...), custom_call_target="tpu_custom_call" | custom-call | tf_op jit(solution)/shard_map/gauss_newton/pallas_call | solution.py:340
  56.0 0.7 %convert.1 = f32[8,64,128]{2,1,0:T(8,128)} convert(bf16[8,64,128]{2,1,0:T(8,128)(2,1)S(1)} %bitcast.7) | non-fusion elementwise | flops 65536 | bytes 393216 | tf_op jit(solution)/shard_map/reshape | solution.py:372
  56.8 0.6 %copy.10 = f32[1,4,2,128]{3,2,1,0:T(2,128)} copy(f32[1,4,2,128]{3,2,1,0:T(2,128)S(1)} %bitcast.9) | data formatting | bytes 8192
Async XLA Ops:
  0.6 0.7 %copy-start.2 = (f32[1,4,2,128]{3,2,1,0:T(2,128)S(1)}, f32[1,4,2,128]{3,2,1,0:T(2,128)}, u32[]{:S(2)}) copy-start(f32[1,4,2,128]{3,2,1,0:T(2,128)} %param.7) | copy-start | bytes 12292
  0.6 0.7 %copy-start.5 = (f32[1,4]{1,0:T(1,128)S(1)}, f32[1,4]{1,0:T(1,128)}, u32[]{:S(2)}) copy-start(f32[1,4]{1,0:T(1,128)} %noise_hbm.1) | copy-start | bytes 52
  0.7 0.7 %copy-start.6 = (f32[16]{0:T(128)S(1)}, f32[16]{0:T(128)}, u32[]{:S(2)}) copy-start(f32[16]{0:T(128)} %param.12) | copy-start | bytes 196
  1.3 1.2 %copy-start = (bf16[1,8,64,2,512]{4,3,2,1,0:T(2,128)(2,1)S(1)}, bf16[1,8,64,2,512]{4,3,2,1,0:T(2,128)(2,1)}, u32[]{:S(2)}) copy-start(bf16[1,8,64,2,512]{4,3,2,1,0:T(2,128)(2,1)} %param.9) | copy-start | bytes 3145732
  2.6 0.9 %copy-start.1 = (f32[8,64,128]{2,1,0:T(8,128)S(1)}, f32[8,64,128]{2,1,0:T(8,128)}, u32[]{:S(2)}) copy-start(f32[8,64,128]{2,1,0:T(8,128)} %m_hbm.1) | copy-start | bytes 786436
  3.5 0.7 %copy-start.3 = (s32[8,64]{1,0:T(8,128)S(1)}, s32[8,64]{1,0:T(8,128)}, u32[]{:S(2)}) copy-start(s32[8,64]{1,0:T(8,128)} %cls_hbm.1) | copy-start | bytes 6148
  4.2 0.7 %copy-start.4 = (f32[4,16]{1,0:T(4,128)S(1)}, f32[4,16]{1,0:T(4,128)}, u32[]{:S(2)}) copy-start(f32[4,16]{1,0:T(4,128)} %coup_hbm.1) | copy-start | bytes 772

commit v2 on v1

--- a/solution.py
+++ b/solution.py
@@ -25,8 +25,8 @@
     wout, gout,
     kscr, ext, obs_v, noise_v, cls_in, kappa_v, coup_v,
     mx, p, cin, onout, onin, xin, b, yin, zout, zin, wf, wt, wtin,
-    g, fsend, fin, fown, va, vb, coef, cls,
-    lsem, csem, xsem, ysem, zsem, osem, aysem, axsem, acsem, tsem, rsem, gsem, hsem,
+    g, fsend, fin, fsum, fown, va, vb, coef, cls,
+    lsem, csem, xsem, ysem, zsem, osem, aysem, acsem, tsem, rsem, gsem, hsem, ready,
 ):
     f = lax.axis_index("freq")
     px = lax.axis_index("px")
@@ -41,10 +41,13 @@
     x_peers = [dev(x=(x + d) % NX_CHIP) for d in range(1, NX_CHIP)]
     y_peers = [dev(y=(y + d) % NY_CHIP) for d in range(1, NY_CHIP)]
     z_peer = dev(zh=1 - zh)
+    far_y = (4, 3, 5, 2, 6, 1, 7, 0)
+    yz_steps = [(d, e) for e in (1, 0) for d in far_y if (d, e) != (0, 0)]
+    yz_peers = [dev(y=(y + d) % NY_CHIP, zh=(zh + e) % NZ) for d, e in yz_steps]
+    xy_steps = [(a, d) for d in far_y for a in (2, 1, 3, 0) if (a, d) != (0, 0)]
+    xy_peers = [dev(x=(x + a) % NX_CHIP, y=(y + d) % NY_CHIP) for a, d in xy_steps]
     f_peers = [dev(f=(f + d) % NF) for d in range(1, NF)]
     npx, npy = NZ * NY_CHIP, NX_CHIP * 2
-    above = {"freq": f, "px": (px + npx - 1) % npx, "py": py}
-    below = {"freq": f, "px": (px + 1) % npx, "py": py}
     left = {"freq": f, "px": px, "py": (py + npy - 1) % npy}
     right = {"freq": f, "px": px, "py": (py + 1) % npy}
 
@@ -61,7 +64,7 @@
     ]
 
     bar = pltpu.get_barrier_semaphore()
-    greeted = [partner, left, right, z_peer, above, below] + x_peers + y_peers + f_peers
+    greeted = [partner, left, right, z_peer] + x_peers + y_peers + f_peers
     for peer in greeted:
         pl.semaphore_signal(bar, inc=1, device_id=peer, device_id_type=MESH)
 
@@ -108,11 +111,13 @@
         rows = pl.ds(lb * 4, 4)
         p[0, rows] = part[:, :128].reshape(4, 4, 8, 128)
         p[1, rows] = part[:, 128:].reshape(4, 4, 8, 128)
-        if lb == 0:
-            pl.semaphore_wait(bar, len(greeted))
+    pl.semaphore_wait(bar, len(greeted))
+    for lb in range(4):
+        rows = pl.ds(lb * 4, 4)
         copy = remote(p.at[1 - c, rows], cin.at[rows], csem, lb, partner)
         copy.start()
         c_copies.append(copy)
+    pl.semaphore_signal(ready, inc=1, device_id=z_peer, device_id_type=MESH)
     on_copy = remote(onout, onin, osem, 0, partner)
     on_copy.start()
 
@@ -139,16 +144,25 @@
             hsem, 1, v_peer,
         ),
     ]
+    pl.semaphore_wait(ready, 1)
     for copy in v_copies:
         copy.start()
 
+    on_copy.wait_recv()
+    zout[...] = noise_tile + onin[1]
+    n_copy = remote(zout, zin, zsem, 0, z_peer)
+    n_copy.start()
+    obs_chip = obs_own + onin[0]
+
     for copy in x_copies:
         copy.wait_recv()
     b[...] = (p[c, :, x] + xin[0] + (xin[1] + xin[2])).reshape(NZ, NY_CHIP, 8, 128)
 
+    b[zh, y] = b[zh, y] - obs_chip
+
     y_copies = []
-    for d in range(1, NY_CHIP):
-        copy = remote(b.at[:, (y + d) % NY_CHIP], yin.at[d - 1], ysem, d - 1, y_peers[d - 1])
+    for i, (d, e) in enumerate(yz_steps):
+        copy = remote(b.at[:, (y + d) % NY_CHIP], yin.at[i], ysem, i, yz_peers[i])
         copy.start()
         y_copies.append(copy)
 
@@ -165,26 +179,17 @@
     for copy in h_copies:
         copy.start()
 
-    on_copy.wait_recv()
-    noise_chip = noise_tile + onin[1]
-    obs_chip = obs_own + onin[0]
-
+    n_copy.wait_recv()
     for copy in y_copies:
         copy.wait_recv()
-    s01, s23, s45 = yin[0] + yin[1], yin[2] + yin[3], yin[4] + yin[5]
-    d_sum = (b[:, y] + yin[6]) + (s01 + s23) + s45
-    for zi in range(NZ):
-        zout[zi] = d_sum[zi] - jnp.where(zh == zi, obs_chip, 0.0)
-    zout[2] = noise_chip
-
-    z_copy = remote(zout, zin, zsem, 0, z_peer)
-    z_copy.start()
-    z_copy.wait_recv()
+    terms = [b[:, y]] + [yin[i] for i in range(len(yz_steps))]
+    while len(terms) > 1:
+        terms = [u + v for u, v in zip(terms[::2], terms[1::2])]
 
     w_own = jnp.zeros((8, 128), F32)
     for zi in range(NZ):
-        misfit = zout[zi] + zin[zi]
-        noise = jnp.where(zh == zi, noise_chip, zin[2])
+        misfit = terms[0][zi]
+        noise = jnp.where(zh == zi, zout[...], zin[...])
         inverse = 1.0 / (noise * noise)
         square = misfit * misfit
         spread = (square + rolled(square, 64, 1)) * inverse
@@ -193,11 +198,11 @@
         w_own = jnp.where(zh == zi, weighted, w_own)
     wt[...] = w_own
 
-    ay_copies = []
-    for d in range(1, NY_CHIP):
-        copy = remote(wf.at[c, :, y, x], wf.at[c, :, y, x], aysem, d - 1, y_peers[d - 1])
-        copy.start()
-        ay_copies.append(copy)
+    a_copies = {}
+    for i, (a, d) in enumerate(xy_steps):
+        copy = remote(wf.at[c, :, y, x], wf.at[c, :, y, x], aysem, i, xy_peers[i])
+        copy.start()
+        a_copies[a, d] = copy
     t_copy = remote(wt, wtin, tsem, 0, partner)
     t_copy.start()
 
@@ -257,23 +262,15 @@
 
         lax.fori_loop(1 + sweep, 9 - sweep, row_step, 0)
         src, dst = dst, src
-    prior = PRIOR_WEIGHT * src[4:6, 8:72, :].reshape(128, 128)
-    fown[...] = prior
-
-    for copy in ay_copies:
-        copy.wait_recv()
-    own_x = wf.at[c, :, :, x]
-    ax_copies = []
-    for d in range(1, NX_CHIP):
-        copy = remote(own_x, own_x, axsem, d - 1, x_peers[d - 1])
-        copy.start()
-        ax_copies.append(copy)
-    ac_copies = [remote(own_x, own_x, acsem, 0, partner)]
-    ac_copies[0].start()
-    for d in (1, 3, 2):
-        ax_copies[d - 1].wait_recv()
-        from_x = wf.at[c, :, :, (x + NX_CHIP - d) % NX_CHIP]
-        copy = remote(from_x, from_x, acsem, d, partner)
+    fown[...] = PRIOR_WEIGHT * src[4:6, 8:72, :]
+
+    ac_copies = []
+    for i, a in enumerate((0, 1, 3, 2)):
+        for d in far_y[::-1]:
+            if (a, d) in a_copies:
+                a_copies[a, d].wait_recv()
+        column_x = wf.at[c, :, :, (x + NX_CHIP - a) % NX_CHIP]
+        copy = remote(column_x, column_x, acsem, i, partner)
         copy.start()
         ac_copies.append(copy)
 
@@ -292,43 +289,50 @@
         [wf.at[h].reshape(512, 128)[...] for h in range(2)], axis=1
     )
 
-    lo128 = lax.broadcasted_iota(jnp.int32, (128, 128), 1) < 64
-    r_copies = []
-    for d in (2, 3, 1, 0):
-        q = (f + d) % NF
-        rows = pl.ds(pl.multiple_of(q * 256, 256), 256)
-        kq = jnp.concatenate([kscr.at[lb].reshape(1024, 128)[rows, :] for lb in range(4)], axis=1)
-        both = jnp.dot(kq, weights, preferred_element_type=F32)
-        g[0] = both[:, :128]
-        g[1] = both[:, 128:]
-        e0, o0 = g.at[0][pl.ds(0, 128, stride=2), :], g.at[0][pl.ds(1, 128, stride=2), :]
-        e1, o1 = g.at[1][pl.ds(0, 128, stride=2), :], g.at[1][pl.ds(1, 128, stride=2), :]
-        grad = jnp.where(lo128, e0, o1) + rolled(jnp.where(lo128, e1, o0), 64, 1)
-        if d:
-            fsend[d - 1] = grad.astype(BF16)
-            copy = remote(fsend.at[d - 1], fin.at[d - 1], rsem, d - 1, f_peers[d - 1])
+    lo64 = lax.broadcasted_iota(jnp.int32, (64, 128), 1) < 64
+    steps = (3, 2, 1, 0)
+    r_copies, totals = [[], []], []
+    for h in range(2):
+        kq = []
+        for d in steps:
+            rows = pl.ds(pl.multiple_of((f + d) % NF * 256 + h * 128, 128), 128)
+            kq.append(jnp.concatenate([kscr.at[lb].reshape(1024, 128)[rows, :] for lb in range(4)], axis=1))
+        both = jnp.dot(jnp.concatenate(kq, axis=0), weights, preferred_element_type=F32)
+        g[h, 0] = both[:, :128]
+        g[h, 1] = both[:, 128:]
+        for i, d in enumerate(steps):
+            e0, o0, e1, o1 = [
+                g.at[h, half][pl.ds(i * 128 + odd_row, 64, stride=2), :] for half in range(2) for odd_row in range(2)
+            ]
+            grad = jnp.where(lo64, e0, o1) + rolled(jnp.where(lo64, e1, o0), 64, 1)
+            if d:
+                fsend[d - 1, h] = grad.astype(BF16)
+                copy = remote(fsend.at[d - 1, h], fin.at[d - 1, h], rsem, (d - 1) * 2 + h, f_peers[d - 1])
+                copy.start()
+                r_copies[h].append(copy)
+            else:
+                totals.append(grad + fown[h])
+    g_copies, own = [], []
+    for h in range(2):
+        for copy in r_copies[h]:
+            copy.wait_recv()
+        total = totals[h] + (fin[0, h].astype(F32) + fin[1, h].astype(F32)) + fin[2, h].astype(F32)
+        fsum[h] = total.astype(BF16)
+        row = gout.at[2 * f + h]
+        for d in (3, 2, 1):
+            copy = remote(fsum.at[h], row, gsem, (d - 1) * 2 + h, f_peers[d - 1])
             copy.start()
-            r_copies.append(copy)
-        else:
-            total = grad + fown[...]
-    for copy in r_copies:
-        copy.wait_recv()
-    total = total + (fin[0].astype(F32) + fin[1].astype(F32)) + fin[2].astype(F32)
-    fsum = fsend.at[3]
-    fsum[...] = total.astype(BF16)
-    own = pltpu.make_async_copy(fsum, gout.at[f], lsem.at[10])
-    own.start()
-    g_copies = []
-    for d in range(1, NF):
-        copy = remote(fsum, gout.at[f], gsem, d - 1, f_peers[d - 1])
-        copy.start()
-        g_copies.append(copy)
+            g_copies.append(copy)
+        copy = pltpu.make_async_copy(fsum.at[h], row, lsem.at[10 + h])
+        copy.start()
+        own.append(copy)
     for copy in g_copies:
         copy.wait_recv()
-    own.wait()
+    for copy in own:
+        copy.wait()
     everything = (
-        c_copies + [on_copy] + x_copies + v_copies + y_copies + h_copies + [z_copy] + ay_copies
-        + [t_copy] + ax_copies + ac_copies + r_copies + g_copies
+        c_copies + [on_copy, n_copy] + x_copies + v_copies + y_copies + h_copies + list(a_copies.values())
+        + [t_copy] + ac_copies + r_copies[0] + r_copies[1] + g_copies
     )
     for copy in everything:
         copy.wait_send()
@@ -342,25 +346,25 @@
         name="gauss_newton",
         out_shape=(
             jax.ShapeDtypeStruct((8, 128), F32),
-            jax.ShapeDtypeStruct((NF, 128, 128), BF16),
+            jax.ShapeDtypeStruct((8, 64, 128), BF16),
         ),
-        in_specs=[pl.BlockSpec(memory_space=pl.ANY)] * 7,
+        in_specs=[pl.BlockSpec(memory_space=pltpu.HBM)] * 7,
         out_specs=(pl.BlockSpec(memory_space=pltpu.VMEM), pl.BlockSpec(memory_space=pl.ANY)),
         scratch_shapes=[
             vmem((4, 512, 2, 128), BF16), vmem((16, 80, 128)), vmem((8, 128)), vmem((1, 4)),
             vmem((3, 24, 64), jnp.int32), vmem((1, 16)), vmem((4, 16)),
             vmem((2, 1024, 128)), vmem((2, 16, 4, 8, 128)), vmem((16, 4, 8, 128)), vmem((2, 8, 128)), vmem((2, 8, 128)),
-            vmem((3, 16, 8, 128)), vmem((2, 8, 8, 128)), vmem((7, 2, 8, 128)), vmem((3, 8, 128)), vmem((3, 8, 128)),
+            vmem((3, 16, 8, 128)), vmem((2, 8, 8, 128)), vmem((15, 2, 8, 128)), vmem((8, 128)), vmem((8, 128)),
             vmem((2, 2, 8, 4, 8, 128), BF16), vmem((8, 128)), vmem((8, 128)),
-            vmem((2, 256, 128)), vmem((4, 128, 128), BF16), vmem((3, 128, 128), BF16), vmem((128, 128)),
+            vmem((2, 2, 512, 128)), vmem((3, 2, 64, 128), BF16), vmem((3, 2, 64, 128), BF16), vmem((2, 64, 128), BF16), vmem((2, 64, 128)),
             vmem((10, 80, 128)), vmem((10, 80, 128)), vmem((8, 5, 80, 128)), vmem((8, 128), jnp.int32),
-            pltpu.SemaphoreType.DMA((11,)), sems(4), sems(12), sems(7), sems(1), sems(1), sems(7), sems(3), sems(4),
-            sems(1), sems(3), sems(3), sems(6),
+            pltpu.SemaphoreType.DMA((12,)), sems(4), sems(12), sems(15), sems(1), sems(1), sems(31), sems(4), sems(1),
+            sems(6), sems(6), sems(6), pltpu.SemaphoreType.REGULAR,
         ],
         compiler_params=pltpu.CompilerParams(
             collective_id=0, has_side_effects=True, vmem_limit_bytes=48 * 1024 * 1024
         ),
-    )(
+    )(*(pltpu.with_memory_space_constraint(a, pltpu.HBM) for a in (
         forward_kernel.reshape(512, 2, 512),
         model_field,
         observed.reshape(8, 128),
@@ -368,8 +372,8 @@
         classes,
         kappa_table.reshape(1, 16),
         coupling_table,
-    )
-    return weighted.reshape(observed.shape), grad.astype(F32).reshape(model_field.shape)
+    )))
+    return weighted.reshape(observed.shape), grad.astype(F32)
 
 
 def solution(mesh):

time: 57.6 us -> 49.1 us (0.85)
  local copies, waits for them, and re-layouts: 4.8 us -> 0.59 us
  Pallas kernels: 51.2 us -> 47 us
    unnamed x15 -> x1, local copies, waits for them, and re-layouts: 4.8 us -> 0.59 us
    pallas_call x1, Pallas kernels: 51.2 us -> 47 us  [local(): pl.pallas_call(kernel, name='gauss_newton', out_shape=(jax.ShapeDtypeStru...]
    convert_element_type x0 -> x1, other arithmetic: none -> 0.72 us  [local(): return (weighted.reshape(observed.shape), grad.astype(F32))]
    reshape x1 -> x0, other arithmetic: 0.72 us -> none  [local(): grad.astype(F32).reshape(model_field.shape)]
where the time goes in v2:
time: 49.1 us; the launch traced here: 49 us
  Pallas kernels  47 us (96%)
  other arithmetic  0.72 us (1%)
  between operations  0.64 us (1%)
  local copies, waits for them, and re-layouts  0.59 us (1%)
    pallas_call x1, Pallas kernels, local(): pl.pallas_call(kernel, name='gauss_newton', out_shape=(jax.ShapeDtypeStru...  47 us

profile of v2, /device:TPU:1, one launch (start us, length us, event | category | flops | bytes accessed | tf_op | source)
XLA Modules:
  0.0 49.0 jit_solution(6941670612306656421)
XLA Ops:
  0.6 47.0 %gauss_newton.1 = (f32[8,128]{1,0:T(8,128)S(1)}, bf16[8,64,128]{2,1,0:T(8,128)(2,1)S(1)}) custom-call(bf16[512,2,512]{2,1,0:T(2,128)(2,1)} %bitcast.5, f32[8,64,128]{2,1,0:T(8,128)} %m_hbm.1, f32[8,128]{1,0:T(8,128)} %bitcast.6, f32[1,4]{1,0:T(1,128)} %noise_hbm.1, s32[8,64]{1,0:T(8,128)} %cls_hbm.1, f32[1,16]{1,0:T(1,128)} %bitcast.7, f32[4,16]{1,0:T(4,128)} %coup_hbm.1), custom_call_target="tpu_custom_call" | custom-call | tf_op jit(solution)/shard_map/gauss_newton/pallas_call | solution.py:344
  47.7 0.7 %convert_element_type.3 = f32[8,64,128]{2,1,0:T(8,128)} convert(bf16[8,64,128]{2,1,0:T(8,128)(2,1)S(1)} %get-tuple-element.5) | non-fusion elementwise | flops 65536 | bytes 393216 | tf_op jit(solution)/shard_map/convert_element_type | solution.py:376
  48.4 0.6 %copy.10 = f32[1,4,2,128]{3,2,1,0:T(2,128)} copy(f32[1,4,2,128]{3,2,1,0:T(2,128)S(1)} %bitcast.4) | data formatting | bytes 8192

commit v3 on v2

--- a/solution.py
+++ b/solution.py
@@ -23,7 +23,7 @@
 def kernel(
     k_hbm, m_hbm, obs_hbm, noise_hbm, cls_hbm, kappa_hbm, coup_hbm,
     wout, gout,
-    kscr, ext, obs_v, noise_v, cls_in, kappa_v, coup_v,
+    kscr, ext, vsend, vrecv, obs_v, noise_v, cls_in, kappa_v, coup_v,
     mx, p, cin, onout, onin, xin, b, yin, zout, zin, wf, wt, wtin,
     g, fsend, fin, fsum, fown, va, vb, coef, cls,
     lsem, csem, xsem, ysem, zsem, osem, aysem, acsem, tsem, rsem, gsem, hsem, ready,
@@ -39,7 +39,6 @@
 
     partner = dev(c=1 - c)
     x_peers = [dev(x=(x + d) % NX_CHIP) for d in range(1, NX_CHIP)]
-    y_peers = [dev(y=(y + d) % NY_CHIP) for d in range(1, NY_CHIP)]
     z_peer = dev(zh=1 - zh)
     far_y = (4, 3, 5, 2, 6, 1, 7, 0)
     yz_steps = [(d, e) for e in (1, 0) for d in far_y if (d, e) != (0, 0)]
@@ -64,7 +63,15 @@
     ]
 
     bar = pltpu.get_barrier_semaphore()
-    greeted = [partner, left, right, z_peer] + x_peers + y_peers + f_peers
+    zc = zh * NF + f
+
+    def zdev(k):
+        z = (zc + k) % (NZ * NF)
+        return dev(f=z % NF, zh=z // NF)
+
+    two_off = [dev(y=(y + k) % NY_CHIP) for k in (2, NY_CHIP - 2)] + [zdev(k) for k in (2, NZ * NF - 2)]
+    one_off = [dev(y=(y + k) % NY_CHIP) for k in (1, NY_CHIP - 1)] + [zdev(k) for k in (1, NZ * NF - 1)]
+    greeted = [partner, left, right] + x_peers + one_off + two_off
     for peer in greeted:
         pl.semaphore_signal(bar, inc=1, device_id=peer, device_id_type=MESH)
 
@@ -103,6 +110,8 @@
     onout[1] = noise_tile
     obs_own = jnp.where(c == 0, obs_tiles[0], obs_tiles[1])
 
+    vsend[...] = ext[pl.ds(jnp.where(f < 2, 8, 4), 4), 8:72, :].astype(BF16)
+
     c_copies = []
     for lb in range(4):
         k_loads[lb].wait()
@@ -111,63 +120,72 @@
         rows = pl.ds(lb * 4, 4)
         p[0, rows] = part[:, :128].reshape(4, 4, 8, 128)
         p[1, rows] = part[:, 128:].reshape(4, 4, 8, 128)
-    pl.semaphore_wait(bar, len(greeted))
-    for lb in range(4):
-        rows = pl.ds(lb * 4, 4)
+        if lb == 0:
+            pl.semaphore_wait(bar, len(greeted))
+            for peer in two_off:
+                pl.semaphore_signal(ready.at[0], inc=1, device_id=peer, device_id_type=MESH)
         copy = remote(p.at[1 - c, rows], cin.at[rows], csem, lb, partner)
         copy.start()
         c_copies.append(copy)
-    pl.semaphore_signal(ready, inc=1, device_id=z_peer, device_id_type=MESH)
     on_copy = remote(onout, onin, osem, 0, partner)
     on_copy.start()
 
-    x_copies = []
-    for lb in range(4):
-        rows = pl.ds(lb * 4, 4)
-        c_copies[lb].wait_recv()
-        p[c, rows] = p[c, rows] + cin[rows]
-        for d in range(1, NX_CHIP):
-            copy = remote(
-                p.at[c, rows, (x + d) % NX_CHIP], xin.at[d - 1, rows], xsem, (d - 1) * 4 + lb, x_peers[d - 1]
-            )
-            copy.start()
-            x_copies.append(copy)
-
     upper = f < 2
-    src_row = jnp.where(upper, 8, 4)
     dst_row = jnp.where(upper, 0, 12)
+    crosses = (y == jnp.where(upper, NY_CHIP - 1, 0))
     v_peer = {"freq": f, "px": (px + jnp.where(upper, 1, npx - 1)) % npx, "py": py}
     v_copies = [
-        remote(ext.at[pl.ds(src_row, 4), 8:72], ext.at[pl.ds(dst_row, 4), 8:72], hsem, 0, v_peer),
+        remote(vsend, vrecv, hsem, 0, v_peer),
         remote(
             cls_in.at[1, 8:16], cls_in.at[1, pl.ds(pl.multiple_of(jnp.where(upper, 0, 16), 8), 8)],
             hsem, 1, v_peer,
         ),
     ]
-    pl.semaphore_wait(ready, 1)
-    for copy in v_copies:
-        copy.start()
-
+
+    def send_edges():
+        for copy in v_copies:
+            copy.start()
+
+    pl.when(jnp.logical_not(crosses))(send_edges)
+
+    x_copies = {}
+    for lb in range(4):
+        rows = pl.ds(lb * 4, 4)
+        c_copies[lb].wait_recv()
+        p[c, rows] = p[c, rows] + cin[rows]
+        for d in (2, 1, 3):
+            copy = remote(
+                p.at[c, rows, (x + d) % NX_CHIP], xin.at[d - 1, rows], xsem, (d - 1) * 4 + lb, x_peers[d - 1]
+            )
+            copy.start()
+            x_copies[d, lb] = copy
+
+    pl.semaphore_wait(ready.at[0], len(two_off))
+    pl.semaphore_signal(ready.at[1], inc=1, device_id=z_peer, device_id_type=MESH)
     on_copy.wait_recv()
     zout[...] = noise_tile + onin[1]
     n_copy = remote(zout, zin, zsem, 0, z_peer)
     n_copy.start()
     obs_chip = obs_own + onin[0]
-
-    for copy in x_copies:
-        copy.wait_recv()
-    b[...] = (p[c, :, x] + xin[0] + (xin[1] + xin[2])).reshape(NZ, NY_CHIP, 8, 128)
-
-    b[zh, y] = b[zh, y] - obs_chip
+    pl.semaphore_wait(ready.at[1], 1)
+    pl.when(crosses)(send_edges)
 
     y_copies = []
-    for i, (d, e) in enumerate(yz_steps):
-        copy = remote(b.at[:, (y + d) % NY_CHIP], yin.at[i], ysem, i, yz_peers[i])
-        copy.start()
-        y_copies.append(copy)
+    for zi in range(NZ):
+        for (d, lb), copy in x_copies.items():
+            if lb // 2 == zi:
+                copy.wait_recv()
+        half = pl.ds(zi * NY_CHIP, NY_CHIP)
+        b[zi] = p[c, half, x] + xin[0, half] + (xin[1, half] + xin[2, half])
+        b[zi, y] = b[zi, y] - jnp.where(zh == zi, obs_chip, 0.0)
+        for i, (d, e) in enumerate(yz_steps):
+            copy = remote(b.at[zi, (y + d) % NY_CHIP], yin.at[i, zi], ysem, i * NZ + zi, yz_peers[i])
+            copy.start()
+            y_copies.append(copy)
 
     for copy in v_copies:
         copy.wait_recv()
+    ext[pl.ds(dst_row, 4), 8:72, :] = vrecv[...].astype(F32)
     rows10 = pl.ds(2 * f, 10)
     rows16 = pl.ds(pl.multiple_of(jnp.where(upper, 0, 8), 8), 16)
     h_copies = [
@@ -331,11 +349,16 @@
     for copy in own:
         copy.wait()
     everything = (
-        c_copies + [on_copy, n_copy] + x_copies + v_copies + y_copies + h_copies + list(a_copies.values())
+        c_copies + [on_copy, n_copy] + list(x_copies.values()) + v_copies + y_copies + h_copies + list(a_copies.values())
         + [t_copy] + ac_copies + r_copies[0] + r_copies[1] + g_copies
     )
     for copy in everything:
         copy.wait_send()
+
+
+def finish(weighted_ref, grad_ref, weighted_out, grad_out):
+    weighted_out[...] = weighted_ref[...]
+    grad_out[...] = grad_ref[...].astype(F32)
 
 
 def local(observed, noise_scale, forward_kernel, model_field, classes, kappa_table, coupling_table):
@@ -351,15 +374,16 @@
         in_specs=[pl.BlockSpec(memory_space=pltpu.HBM)] * 7,
         out_specs=(pl.BlockSpec(memory_space=pltpu.VMEM), pl.BlockSpec(memory_space=pl.ANY)),
         scratch_shapes=[
-            vmem((4, 512, 2, 128), BF16), vmem((16, 80, 128)), vmem((8, 128)), vmem((1, 4)),
+            vmem((4, 512, 2, 128), BF16), vmem((16, 80, 128)), vmem((4, 64, 128), BF16), vmem((4, 64, 128), BF16),
+            vmem((8, 128)), vmem((1, 4)),
             vmem((3, 24, 64), jnp.int32), vmem((1, 16)), vmem((4, 16)),
             vmem((2, 1024, 128)), vmem((2, 16, 4, 8, 128)), vmem((16, 4, 8, 128)), vmem((2, 8, 128)), vmem((2, 8, 128)),
             vmem((3, 16, 8, 128)), vmem((2, 8, 8, 128)), vmem((15, 2, 8, 128)), vmem((8, 128)), vmem((8, 128)),
             vmem((2, 2, 8, 4, 8, 128), BF16), vmem((8, 128)), vmem((8, 128)),
             vmem((2, 2, 512, 128)), vmem((3, 2, 64, 128), BF16), vmem((3, 2, 64, 128), BF16), vmem((2, 64, 128), BF16), vmem((2, 64, 128)),
             vmem((10, 80, 128)), vmem((10, 80, 128)), vmem((8, 5, 80, 128)), vmem((8, 128), jnp.int32),
-            pltpu.SemaphoreType.DMA((12,)), sems(4), sems(12), sems(15), sems(1), sems(1), sems(31), sems(4), sems(1),
-            sems(6), sems(6), sems(6), pltpu.SemaphoreType.REGULAR,
+            pltpu.SemaphoreType.DMA((12,)), sems(4), sems(12), sems(30), sems(1), sems(1), sems(31), sems(4), sems(1),
+            sems(6), sems(6), sems(6), pltpu.SemaphoreType.REGULAR((2,)),
         ],
         compiler_params=pltpu.CompilerParams(
             collective_id=0, has_side_effects=True, vmem_limit_bytes=48 * 1024 * 1024
@@ -373,7 +397,13 @@
         kappa_table.reshape(1, 16),
         coupling_table,
     )))
-    return weighted.reshape(observed.shape), grad.astype(F32)
+    weighted, grad = pl.pallas_call(
+        finish,
+        name="finish",
+        compiler_params=pltpu.CompilerParams(vmem_limit_bytes=4 * 1024 * 1024),
+        out_shape=(jax.ShapeDtypeStruct(weighted.shape, F32), jax.ShapeDtypeStruct(grad.shape, F32)),
+    )(weighted, grad)
+    return weighted.reshape(observed.shape), grad
 
 
 def solution(mesh):

time: 49.1 us -> 47.7 us (0.971)
  other arithmetic: 0.72 us -> 0 us
  local copies, waits for them, and re-layouts: 0.59 us -> 0 us
    pallas_call x1, Pallas kernels: 47 us -> 46.2 us  [local(): pl.pallas_call(kernel, name='gauss_newton', out_shape=(jax.ShapeDtypeStru...]
    pallas_call x0 -> x1, Pallas kernels: none -> 0.72 us  [local(): pl.pallas_call(finish, name='finish', compiler_params=pltpu.CompilerParam...]
    convert_element_type x1 -> x0, other arithmetic: 0.72 us -> none  [local(): return (weighted.reshape(observed.shape), grad.astype(F32))]
    unnamed x1 -> x0, local copies, waits for them, and re-layouts: 0.59 us -> none
where the time goes in v3:
time: 47.7 us; the launch traced here: 47.6 us
  Pallas kernels  47 us (99%)
  between operations  0.64 us (1%)
    pallas_call x1, Pallas kernels, local(): pl.pallas_call(kernel, name='gauss_newton', out_shape=(jax.ShapeDtypeStru...  46.2 us

profile of v3, /device:TPU:1, one launch (start us, length us, event | category | flops | bytes accessed | tf_op | source)
XLA Modules:
  0.0 47.6 jit_solution(14026298970101593974)
XLA Ops:
  0.6 46.2 %gauss_newton.1 = (f32[8,128]{1,0:T(8,128)S(1)}, bf16[8,64,128]{2,1,0:T(8,128)(2,1)S(1)}) custom-call(bf16[512,2,512]{2,1,0:T(2,128)(2,1)} %bitcast.4, f32[8,64,128]{2,1,0:T(8,128)} %m_hbm.1, f32[8,128]{1,0:T(8,128)} %bitcast.5, f32[1,4]{1,0:T(1,128)} %noise_hbm.1, s32[8,64]{1,0:T(8,128)} %cls_hbm.1, f32[1,16]{1,0:T(1,128)} %bitcast.6, f32[4,16]{1,0:T(4,128)} %coup_hbm.1), custom_call_target="tpu_custom_call" | custom-call | tf_op jit(solution)/shard_map/gauss_newton/pallas_call | solution.py:367
  46.9 0.7 %finish.1 = (f32[8,128]{1,0:T(8,128)}, f32[8,64,128]{2,1,0:T(8,128)}) custom-call(f32[8,128]{1,0:T(8,128)S(1)} %get-tuple-element.6.weighted_ref, bf16[8,64,128]{2,1,0:T(8,128)(2,1)S(1)} %get-tuple-element.7.grad_ref), custom_call_target="tpu_custom_call" | custom-call | tf_op jit(solution)/shard_map/finish/pallas_call | solution.py:400

commit v4 on v3

--- a/solution.py
+++ b/solution.py
@@ -23,10 +23,10 @@
 def kernel(
     k_hbm, m_hbm, obs_hbm, noise_hbm, cls_hbm, kappa_hbm, coup_hbm,
     wout, gout,
-    kscr, ext, vsend, vrecv, obs_v, noise_v, cls_in, kappa_v, coup_v,
-    mx, p, cin, onout, onin, xin, b, yin, zout, zin, wf, wt, wtin,
+    kscr, kother, ext, vsend, vrecv, obs_v, noise_v, cls_in, kappa_v, coup_v,
+    mx, p, cin, onout, onin, xin, b, yin, zout, zin, wf, wt, wtin, pout, pin,
     g, fsend, fin, fsum, fown, va, vb, coef, cls,
-    lsem, csem, xsem, ysem, zsem, osem, aysem, acsem, tsem, rsem, gsem, hsem, ready,
+    lsem, csem, xsem, ysem, zsem, osem, aysem, ksem, psem, tsem, rsem, gsem, hsem, ready,
 ):
     f = lax.axis_index("freq")
     px = lax.axis_index("px")
@@ -197,6 +197,9 @@
     for copy in h_copies:
         copy.start()
 
+    k_copy = remote(kscr, kother, ksem, 0, partner)
+    k_copy.start()
+
     n_copy.wait_recv()
     for copy in y_copies:
         copy.wait_recv()
@@ -212,13 +215,13 @@
         square = misfit * misfit
         spread = (square + rolled(square, 64, 1)) * inverse
         weighted = misfit * ((FREEDOM + 2.0) / (FREEDOM + spread) * inverse)
-        wf[c, zi, y, x] = weighted.astype(BF16)
+        wf[zi, y, x] = weighted.astype(BF16)
         w_own = jnp.where(zh == zi, weighted, w_own)
     wt[...] = w_own
 
     a_copies = {}
     for i, (a, d) in enumerate(xy_steps):
-        copy = remote(wf.at[c, :, y, x], wf.at[c, :, y, x], aysem, i, xy_peers[i])
+        copy = remote(wf.at[:, y, x], wf.at[:, y, x], aysem, i, xy_peers[i])
         copy.start()
         a_copies[a, d] = copy
     t_copy = remote(wt, wtin, tsem, 0, partner)
@@ -280,17 +283,18 @@
 
         lax.fori_loop(1 + sweep, 9 - sweep, row_step, 0)
         src, dst = dst, src
-    fown[...] = PRIOR_WEIGHT * src[4:6, 8:72, :]
-
-    ac_copies = []
-    for i, a in enumerate((0, 1, 3, 2)):
-        for d in far_y[::-1]:
-            if (a, d) in a_copies:
-                a_copies[a, d].wait_recv()
-        column_x = wf.at[c, :, :, (x + NX_CHIP - a) % NX_CHIP]
-        copy = remote(column_x, column_x, acsem, i, partner)
-        copy.start()
-        ac_copies.append(copy)
+    lo32 = lax.broadcasted_iota(jnp.int32, (32, 128), 1) < 64
+
+    def packed(lo_half):
+        return jnp.where(lo32, lo_half[:32], rolled(lo_half[32:], 64, 1))
+
+    for h in range(2):
+        prior = PRIOR_WEIGHT * src[4 + h, 8:72, :]
+        turned = rolled(prior, 64, 1)
+        fown[h] = packed(jnp.where(c == 0, prior, turned))
+        pout[h] = packed(jnp.where(c == 0, turned, prior))
+    p_copy = remote(pout, pin, psem, 0, partner)
+    p_copy.start()
 
     t_copy.wait_recv()
     other = wtin[...]
@@ -301,47 +305,50 @@
     wout[pl.ds(0, 4, stride=2), :] = jnp.where(lo4, half0, rolled(half1, 64, 1))
     wout[pl.ds(1, 4, stride=2), :] = jnp.where(lo4, rolled(half0, 64, 1), half1)
 
-    for copy in ac_copies:
+    k_copy.wait_recv()
+    p_copy.wait_recv()
+    for copy in a_copies.values():
         copy.wait_recv()
-    weights = jnp.concatenate(
-        [wf.at[h].reshape(512, 128)[...] for h in range(2)], axis=1
-    )
-
-    lo64 = lax.broadcasted_iota(jnp.int32, (64, 128), 1) < 64
-    steps = (3, 2, 1, 0)
+    weights = wf.reshape(512, 128)[...]
+
     r_copies, totals = [[], []], []
     for h in range(2):
         kq = []
-        for d in steps:
+        for d in (3, 2, 1, 0):
             rows = pl.ds(pl.multiple_of((f + d) % NF * 256 + h * 128, 128), 128)
-            kq.append(jnp.concatenate([kscr.at[lb].reshape(1024, 128)[rows, :] for lb in range(4)], axis=1))
-        both = jnp.dot(jnp.concatenate(kq, axis=0), weights, preferred_element_type=F32)
-        g[h, 0] = both[:, :128]
-        g[h, 1] = both[:, 128:]
-        for i, d in enumerate(steps):
-            e0, o0, e1, o1 = [
-                g.at[h, half][pl.ds(i * 128 + odd_row, 64, stride=2), :] for half in range(2) for odd_row in range(2)
+            kq += [
+                jnp.concatenate([k.at[lb].reshape(1024, 128)[rows, :] for lb in range(4)], axis=1)
+                for k in (kscr, kother)
             ]
-            grad = jnp.where(lo64, e0, o1) + rolled(jnp.where(lo64, e1, o0), 64, 1)
+        g[h] = jnp.dot(jnp.concatenate(kq, axis=0), weights, preferred_element_type=F32).reshape(4, 256, 128)
+        for d in (3, 2, 1, 0):
+            grads = []
+            for k in range(2):
+                e, o = [g.at[h, 3 - d][pl.ds(k * 128 + odd_row, 64, stride=2), :] for odd_row in range(2)]
+                grads.append(packed(e + rolled(o, 64, 1)))
+            grad = jnp.concatenate(grads, axis=0)
             if d:
                 fsend[d - 1, h] = grad.astype(BF16)
                 copy = remote(fsend.at[d - 1, h], fin.at[d - 1, h], rsem, (d - 1) * 2 + h, f_peers[d - 1])
                 copy.start()
                 r_copies[h].append(copy)
             else:
-                totals.append(grad + fown[h])
+                totals.append(grad + jnp.concatenate([fown[h], pin[h]], axis=0))
     g_copies, own = [], []
     for h in range(2):
         for copy in r_copies[h]:
             copy.wait_recv()
         total = totals[h] + (fin[0, h].astype(F32) + fin[1, h].astype(F32)) + fin[2, h].astype(F32)
-        fsum[h] = total.astype(BF16)
-        row = gout.at[2 * f + h]
-        for d in (3, 2, 1):
-            copy = remote(fsum.at[h], row, gsem, (d - 1) * 2 + h, f_peers[d - 1])
-            copy.start()
-            g_copies.append(copy)
-        copy = pltpu.make_async_copy(fsum.at[h], row, lsem.at[10 + h])
+        fsum[h] = total.astype(BF16).reshape(2, 32, 128)
+        row = gout.at[c, 2 * f + h]
+        for d in (3, 2, 1, 0):
+            for k in range(2):
+                if (d, k) != (0, 0):
+                    peer = dev(f=(f + d) % NF, c=(c + k) % 2)
+                    copy = remote(fsum.at[h, k], row, gsem, (d * 2 + k) * 2 + h, peer)
+                    copy.start()
+                    g_copies.append(copy)
+        copy = pltpu.make_async_copy(fsum.at[h, 0], row, lsem.at[10 + h])
         copy.start()
         own.append(copy)
     for copy in g_copies:
@@ -350,7 +357,7 @@
         copy.wait()
     everything = (
         c_copies + [on_copy, n_copy] + list(x_copies.values()) + v_copies + y_copies + h_copies + list(a_copies.values())
-        + [t_copy] + ac_copies + r_copies[0] + r_copies[1] + g_copies
+        + [t_copy, k_copy, p_copy] + r_copies[0] + r_copies[1] + g_copies
     )
     for copy in everything:
         copy.wait_send()
@@ -358,7 +365,10 @@
 
 def finish(weighted_ref, grad_ref, weighted_out, grad_out):
     weighted_out[...] = weighted_ref[...]
-    grad_out[...] = grad_ref[...].astype(F32)
+    first, second = grad_ref[0].astype(F32), grad_ref[1].astype(F32)
+    low = lax.broadcasted_iota(jnp.int32, first.shape, 2) < 64
+    grad_out[:, :32] = jnp.where(low, first, rolled(second, 64, 2))
+    grad_out[:, 32:] = jnp.where(low, rolled(first, 64, 2), second)
 
 
 def local(observed, noise_scale, forward_kernel, model_field, classes, kappa_table, coupling_table):
@@ -369,21 +379,21 @@
         name="gauss_newton",
         out_shape=(
             jax.ShapeDtypeStruct((8, 128), F32),
-            jax.ShapeDtypeStruct((8, 64, 128), BF16),
+            jax.ShapeDtypeStruct((2, 8, 32, 128), BF16),
         ),
         in_specs=[pl.BlockSpec(memory_space=pltpu.HBM)] * 7,
         out_specs=(pl.BlockSpec(memory_space=pltpu.VMEM), pl.BlockSpec(memory_space=pl.ANY)),
         scratch_shapes=[
-            vmem((4, 512, 2, 128), BF16), vmem((16, 80, 128)), vmem((4, 64, 128), BF16), vmem((4, 64, 128), BF16),
+            vmem((4, 512, 2, 128), BF16), vmem((4, 512, 2, 128), BF16), vmem((16, 80, 128)), vmem((4, 64, 128), BF16), vmem((4, 64, 128), BF16),
             vmem((8, 128)), vmem((1, 4)),
             vmem((3, 24, 64), jnp.int32), vmem((1, 16)), vmem((4, 16)),
             vmem((2, 1024, 128)), vmem((2, 16, 4, 8, 128)), vmem((16, 4, 8, 128)), vmem((2, 8, 128)), vmem((2, 8, 128)),
             vmem((3, 16, 8, 128)), vmem((2, 8, 8, 128)), vmem((15, 2, 8, 128)), vmem((8, 128)), vmem((8, 128)),
-            vmem((2, 2, 8, 4, 8, 128), BF16), vmem((8, 128)), vmem((8, 128)),
-            vmem((2, 2, 512, 128)), vmem((3, 2, 64, 128), BF16), vmem((3, 2, 64, 128), BF16), vmem((2, 64, 128), BF16), vmem((2, 64, 128)),
+            vmem((2, 8, 4, 8, 128), BF16), vmem((8, 128)), vmem((8, 128)), vmem((2, 32, 128)), vmem((2, 32, 128)),
+            vmem((2, 4, 256, 128)), vmem((3, 2, 64, 128), BF16), vmem((3, 2, 64, 128), BF16), vmem((2, 2, 32, 128), BF16), vmem((2, 32, 128)),
             vmem((10, 80, 128)), vmem((10, 80, 128)), vmem((8, 5, 80, 128)), vmem((8, 128), jnp.int32),
-            pltpu.SemaphoreType.DMA((12,)), sems(4), sems(12), sems(30), sems(1), sems(1), sems(31), sems(4), sems(1),
-            sems(6), sems(6), sems(6), pltpu.SemaphoreType.REGULAR((2,)),
+            pltpu.SemaphoreType.DMA((12,)), sems(4), sems(12), sems(30), sems(1), sems(1), sems(31), sems(1), sems(1), sems(1),
+            sems(6), sems(16), sems(6), pltpu.SemaphoreType.REGULAR((2,)),
         ],
         compiler_params=pltpu.CompilerParams(
             collective_id=0, has_side_effects=True, vmem_limit_bytes=48 * 1024 * 1024
@@ -401,7 +411,7 @@
         finish,
         name="finish",
         compiler_params=pltpu.CompilerParams(vmem_limit_bytes=4 * 1024 * 1024),
-        out_shape=(jax.ShapeDtypeStruct(weighted.shape, F32), jax.ShapeDtypeStruct(grad.shape, F32)),
+        out_shape=(jax.ShapeDtypeStruct(weighted.shape, F32), jax.ShapeDtypeStruct((8, 64, 128), F32)),
     )(weighted, grad)
     return weighted.reshape(observed.shape), grad
 

time: 47.7 us -> 47.3 us (level)
  Pallas kernels: 47 us -> 46.5 us
    pallas_call x1, Pallas kernels: 46.2 us -> 45.7 us  [local(): pl.pallas_call(kernel, name='gauss_newton', out_shape=(jax.ShapeDtypeStru...]
where the time goes in v4:
time: 47.3 us; the launch traced here: 47.2 us
  Pallas kernels  46.5 us (98%)
  between operations  0.64 us (1%)
    pallas_call x1, Pallas kernels, local(): pl.pallas_call(kernel, name='gauss_newton', out_shape=(jax.ShapeDtypeStru...  45.7 us

profile of v4, /device:TPU:1, one launch (start us, length us, event | category | flops | bytes accessed | tf_op | source)
XLA Modules:
  0.0 47.2 jit_solution(13936024248147736831)
XLA Ops:
  0.6 45.7 %gauss_newton.1 = (f32[8,128]{1,0:T(8,128)S(1)}, bf16[2,8,32,128]{3,2,1,0:T(8,128)(2,1)S(1)}) custom-call(bf16[512,2,512]{2,1,0:T(2,128)(2,1)} %bitcast.4, f32[8,64,128]{2,1,0:T(8,128)} %m_hbm.1, f32[8,128]{1,0:T(8,128)} %bitcast.5, f32[1,4]{1,0:T(1,128)} %noise_hbm.1, s32[8,64]{1,0:T(8,128)} %cls_hbm.1, f32[1,16]{1,0:T(1,128)} %bitcast.6, f32[4,16]{1,0:T(4,128)} %coup_hbm.1), custom_call_target="tpu_custom_call" | custom-call | tf_op jit(solution)/shard_map/gauss_newton/pallas_call | solution.py:377
  46.4 0.8 %finish.1 = (f32[8,128]{1,0:T(8,128)}, f32[8,64,128]{2,1,0:T(8,128)}) custom-call(f32[8,128]{1,0:T(8,128)S(1)} %get-tuple-element.6.weighted_ref, bf16[2,8,32,128]{3,2,1,0:T(8,128)(2,1)S(1)} %get-tuple-element.7.grad_ref), custom_call_target="tpu_custom_call" | custom-call | tf_op jit(solution)/shard_map/finish/pallas_call | solution.py:410
